TPU v7x, 512 devices: a whole 4x8x8 slice. The times are simulated.
512 devices in a mesh: date: 16 (over z, x_hi), trade: 16 (over y, core), path: 2 (over x_lo).
Axes of the slice: x: 4 (x_hi: 2, x_lo: 2; x = x_hi * 2 + x_lo), y: 8, z: 8, core: 2. Of those that a mesh axis runs over, the one named last changes fastest.
Arguments:
- normals: bfloat16 [32, 64, 8192], P('date', None, ('trade', 'path')), may hold values from -6 to 6
- chol: float32 [64, 64], replicated, as said below
- volatility: float32 [64], replicated, may hold values from 0.5 to 2
- start_state: float32 [64], replicated, may hold values from -3 to 3
- basis_map: float32 [64, 128], replicated, may hold values from -0.75 to 0.75
- basis_bias: float32 [128], replicated, may hold values from -3 to 3
- coef: bfloat16 [128, 16384], P(None, 'trade'), may hold values from -0.5 to 0.5
- maturity: int32 [16384], P('trade'), may hold values from 1 to 32
- netting: int32 [16384], P('trade'), may hold values from 0 to 2047, as said below
Outputs:
- exposure: float32 [32, 2048], P('date', 'trade')
Inputs may be any that keep to these rules, and one draw needn't show every extreme that they name: netting sets are whole within a shard of trades: netting[j] // 128 == j // 1024, and every netting set holds at least one trade. `chol`: lower triangular with a positive diagonal.
All inputs are finite; a program needn't handle non-finite values.
Results may differ from a plain program's by a relative error of at most 0.00035.
Values may be sent and summed in bfloat16 or wider, within the bound.
A program may use at most 64 MiB of HBM per device.

v0:
```python
import jax
import jax.numpy as jnp
from jax import lax
from jax.sharding import PartitionSpec as P

NS_DEV = 128


def entering(array, axis, join, neutral):
    place = lax.axis_index(axis)
    gathered = lax.all_gather(array.astype(jnp.bfloat16), axis)
    state = jnp.zeros_like(array) + jnp.asarray(neutral, array.dtype)

    def one(lap, state):
        return join(state, lax.dynamic_index_in_dim(gathered, lap, 0, False).astype(array.dtype))

    return lax.fori_loop(0, place, one, state)


def add_pair(earlier, later):
    return earlier + later


def local_moves(draws, chol, volatility, date_total):
    scale = volatility * jnp.sqrt(jnp.float32(1.0) / date_total)
    moves = jnp.einsum(
        "fg,tgp->tfp", chol, draws.astype(jnp.float32), precision=lax.Precision.HIGHEST
    )
    return jnp.cumsum(moves * scale[None, :, None], axis=0)


def shards(normals, chol, volatility, start_state, basis_map, basis_bias, coef, maturity, netting):
    date_count, factor_count, path_count = normals.shape
    trade_count = coef.shape[1]
    set_count = trade_count * 0 + NS_DEV
    date_total = date_count * lax.axis_size("date")
    path_total = path_count * lax.axis_size("trade") * lax.axis_size("path")
    first_date = lax.axis_index("date") * date_count
    when = first_date + jnp.arange(date_count, dtype=jnp.int32)
    alive = (when[:, None] < maturity[None, :]).astype(jnp.float32)
    local_set = netting - lax.axis_index("trade") * set_count
    member = (local_set[:, None] == jnp.arange(set_count, dtype=jnp.int32)[None, :]).astype(
        jnp.bfloat16
    )
    own_local = local_moves(normals, chol, volatility, date_total)
    empty = jnp.zeros_like(own_local[-1])
    prior = entering(own_local[-1], "date", add_pair, empty)
    states = start_state[None, :, None] + prior[None] + own_local
    pre = jnp.einsum(
        "tfp,fk->tpk",
        lax.all_gather(states, "trade", axis=2, tiled=True),
        basis_map,
        precision=lax.Precision.HIGHEST,
    )
    basis = jnp.tanh(pre + basis_bias[None, None, :]).astype(jnp.bfloat16)
    value = jnp.einsum("tpk,kj->tpj", basis, coef, preferred_element_type=jnp.float32)
    value = (value * alive[:, None, :]).astype(jnp.bfloat16)
    net = jnp.einsum("tpj,js->tps", value, member, preferred_element_type=jnp.float32)
    total = jnp.sum(jnp.maximum(net, 0.0), axis=1)
    summed = lax.psum(total, "path")
    return summed / path_total


def solution(mesh):
    placed = (
        P("date", None, ("trade", "path")),
        P(),
        P(),
        P(),
        P(),
        P(),
        P(None, "trade"),
        P("trade"),
        P("trade"),
    )
    return jax.shard_map(
        shards, mesh=mesh, in_specs=placed, out_specs=P("date", "trade"), check_vma=False
    )
```

profile of v0, /device:TPU:1, one launch (start us, length us, event | category | flops | bytes accessed | tf_op | source)
XLA Modules:
  0.0 125.8 jit_solution(15111759457493451321)
XLA Ops:
  6.5 0.0 copy-start
  6.5 0.0 copy-start.4
  6.5 0.0 copy-start.3
  6.5 0.0 copy-start.2
  6.5 0.0 copy-start.1
  6.5 0.0 copy-start.5
  6.6 0.0 all-gather.2.cloned.1.call-start
  6.6 0.7 broadcast_multiply_fusion.1
  7.3 1.0 fusion.8
  8.4 0.1 fusion.16
  8.5 43.9 %all_gather.7 = bf16[16,64,256]{2,1,0:T(8,128)(2,1)S(1)} all-gather(bf16[1,64,256]{2,1,0:T(8,128)(2,1)S(1)} %slice.7), channel_id=1, replica_groups=mesh['date'=16,'trade'=16,'path'=2] {'date'}, dimensions={0}, use_global_device_ids=true | all-gather | bytes 557056 | tf_op jit(solution)/shard_map/all_gather | solution.py:11
  52.4 0.0 copy-done.4
  52.4 0.1 broadcast_add_fusion.1
  52.5 0.7 broadcast_add_fusion
  53.2 0.0 all-gather.2.cloned.1.call-update
  53.2 0.0 copy-done.3
  53.2 0.0 copy-done.2
  53.2 0.1 compare_convert_fusion
  53.3 43.9 %all-gather.2.cloned.1.call-done = f32[2,64,4096]{2,1,0:T(8,128)} async-done(((f32[2,64,256]{2,1,0:T(8,128)}), f32[2,64,4096]{2,1,0:T(8,128)}) %all-gather.2.cloned.1.call-update) | async-done | bytes 2097168 | tf_op jit(solution)/shard_map/all_gather | solution.py:51
  97.2 0.0 copy-done.1
  97.2 0.0 copy-done.5
  97.2 8.3 %fusion.6 = bf16[2,4096,128]{2,1,0:T(8,128)(2,1)S(1)} fusion(f32[2,64,4096]{2,1,0:T(8,128)} %all-gather.2.cloned.1.call-done, f32[128]{0:T(128)S(1)} %copy-done.5, f32[64,128]{1,0:T(8,128)S(1)} %copy-done.1), kind=kOutput, calls=%fused_computation.8 | convolution fusion | flops 807403520 | bytes 4227584 | tf_op jit(solution)/shard_map/tfp,fk->tpk/dot_general | solution.py:49
  105.5 0.0 copy-done
  105.5 9.0 %fusion.7 = f32[2,128]{1,0:T(2,128)S(1)} fusion(f32[2,1024]{1,0:T(2,128)S(1)} %compare_convert_fusion, bf16[2,4096,128]{2,1,0:T(8,128)(2,1)S(1)} %fusion.6, bf16[128,1024]{1,0:T(8,128)(2,1)S(1)} %copy-done, s32[1024]{0:T(1024)S(1)} %broadcast_subtract_fusion), kind=kOutput, calls=%fused_computation.9 | convolution fusion | flops 4313972736 | bytes 2372608 | tf_op jit(solution)/shard_map/tpj,js->tps/dot_general | solution.py:58
  114.6 3.8 %psum.7 = f32[2,128]{1,0:T(2,128)S(1)} all-reduce(f32[2,128]{1,0:T(2,128)S(1)} %fusion.7), channel_id=1, replica_groups=mesh['date'=16,'trade'=16,'path'=2] {'path'}, use_global_device_ids=true, to_apply=%region_4.5 | all-reduce | flops 256 | bytes 2048 | tf_op jit(solution)/shard_map/psum | solution.py:60
  118.3 0.6 broadcast_multiply_fusion
  (5 shorter events, 0.0 us)
Async XLA Ops:
  6.5 99.0 %copy-start = (bf16[128,1024]{1,0:T(8,128)(2,1)S(1)}, bf16[128,1024]{1,0:T(8,128)(2,1)}, u32[]{:S(2)}) copy-start(bf16[128,1024]{1,0:T(8,128)(2,1)} %param.17) | copy-start | bytes 786436
  6.5 45.9 %copy-start.4 = (f32[64]{0:T(128)S(1)}, f32[64]{0:T(128)}, u32[]{:S(2)}) copy-start(f32[64]{0:T(128)} %param.14) | copy-start | bytes 772
  6.5 46.7 %copy-start.3 = (s32[1024]{0:T(1024)S(1)}, s32[1024]{0:T(1024)}, u32[]{:S(2)}) copy-start(s32[1024]{0:T(1024)} %param.19) | copy-start | bytes 12292
  6.5 46.7 %copy-start.2 = (s32[1024]{0:T(1024)S(1)}, s32[1024]{0:T(1024)}, u32[]{:S(2)}) copy-start(s32[1024]{0:T(1024)} %param.18) | copy-start | bytes 12292
  6.5 90.6 %copy-start.1 = (f32[64,128]{1,0:T(8,128)S(1)}, f32[64,128]{1,0:T(8,128)}, u32[]{:S(2)}) copy-start(f32[64,128]{1,0:T(8,128)} %param.15) | copy-start | bytes 98308
  6.5 90.6 %copy-start.5 = (f32[128]{0:T(128)S(1)}, f32[128]{0:T(128)}, u32[]{:S(2)}) copy-start(f32[128]{0:T(128)} %param.16) | copy-start | bytes 1540
  6.6 90.6 %all-gather.2.cloned.1.call-start = ((), (), s32[]{:S(2)}) async-start(), calls=%async_computation | async-start | bytes 2228224 | tf_op jit(solution)/shard_map/all_gather | solution.py:51
Sparse Core Ops, SparseCore 0:
  53.3 43.8 all-gather.1
where the time goes:
time: 126 us
  blocking collectives  47.7 us (38%)
  waiting for transfers between devices  43.9 us (35%)
  matrix products  18.4 us (15%)
  between operations  13.5 us (11%)
  other arithmetic  2.22 us (2%)
    all_gather x1, blocking collectives, entering(): gathered = lax.all_gather(array.astype(jnp.bfloat16), axis)  43.9 us
    all_gather x1, waiting for transfers between devices, shards(): lax.all_gather(states, 'trade', axis=2, tiled=True)  43.9 us
    dot_general x1, matrix products, shards(): jnp.einsum('tpj,js->tps', value, member, preferred_element_type=jnp.float32)  9.03 us
    dot_general x1, matrix products, shards(): jnp.einsum('tfp,fk->tpk', lax.all_gather(states, 'trade', axis=2, tiled=T...  8.32 us
    psum x1, blocking collectives, shards(): summed = lax.psum(total, 'path')  3.79 us
  transfers between devices with their start and end apart: 1, of which 1 were waited for; matrix products, arithmetic and copies ran while one was open for 0% of the time, Pallas kernels for 0%

commit v1 on v0

--- a/solution.py
+++ b/solution.py
@@ -4,6 +4,22 @@
 from jax.sharding import PartitionSpec as P
 
 NS_DEV = 128
+
+
+def collect(x, axis, dim):
+    ways, here, step = (lax.axis_size(axis), lax.axis_index(axis), x.shape[dim])
+    shape = [n * ways if d == dim else n for d, n in enumerate(x.shape)]
+    full = lax.dynamic_update_slice_in_dim(jnp.zeros(shape, x.dtype), x, here * step, axis=dim)
+    going_up = going_down = x
+    for far in range(1, ways // 2 + 1):
+        going_up = lax.ppermute(going_up, axis, [(d, (d + 1) % ways) for d in range(ways)])
+        full = lax.dynamic_update_slice_in_dim(full, going_up, (here - far) % ways * step, axis=dim)
+        if 2 * far < ways:
+            going_down = lax.ppermute(going_down, axis, [(d, (d - 1) % ways) for d in range(ways)])
+            full = lax.dynamic_update_slice_in_dim(
+                full, going_down, (here + far) % ways * step, axis=dim
+            )
+    return full
 
 
 def entering(array, axis, join, neutral):
@@ -47,10 +63,7 @@
     prior = entering(own_local[-1], "date", add_pair, empty)
     states = start_state[None, :, None] + prior[None] + own_local
     pre = jnp.einsum(
-        "tfp,fk->tpk",
-        lax.all_gather(states, "trade", axis=2, tiled=True),
-        basis_map,
-        precision=lax.Precision.HIGHEST,
+        "tfp,fk->tpk", collect(states, "trade", 2), basis_map, precision=lax.Precision.HIGHEST
     )
     basis = jnp.tanh(pre + basis_bias[None, None, :]).astype(jnp.bfloat16)
     value = jnp.einsum("tpk,kj->tpj", basis, coef, preferred_element_type=jnp.float32)

time: 126 us -> 121 us (0.960)
  the two profiles are of different devices: /device:TPU:1 before, /device:TPU:32 now
where the time goes in v1:
time: 121 us
  blocking collectives  54.8 us (45%)
  waiting for transfers between devices  23.7 us (20%)
  starting transfers between devices  20.7 us (17%)
  matrix products  19.5 us (16%)
  other arithmetic  1.57 us (1%)
    all_gather x1, blocking collectives, entering(): gathered = lax.all_gather(array.astype(jnp.bfloat16), axis)  49.8 us
    ppermute x8, waiting for transfers between devices, collect(): lax.ppermute(going_up, axis, [(d, (d + 1) % ways) for d in range(ways)])  23.7 us
    ppermute x7, starting transfers between devices, collect(): lax.ppermute(going_down, axis, [(d, (d - 1) % ways) for d in range(ways)])  20.7 us
    dot_general x1, matrix products, shards(): jnp.einsum('tpj,js->tps', value, member, preferred_element_type=jnp.float32)  10.6 us
    dot_general x1, matrix products, shards(): jnp.einsum('tfp,fk->tpk', collect(states, 'trade', 2), basis_map, precisi...  7.9 us
    psum x1, blocking collectives, shards(): summed = lax.psum(total, 'path')  4.94 us
  transfers between devices with their start and end apart: 15, of which 8 were waited for; matrix products, arithmetic and copies ran while one was open for 0% of the time, Pallas kernels for 0%

profile of v1, /device:TPU:32, one launch (start us, length us, event | category | flops | bytes accessed | tf_op | source)
XLA Modules:
  0.0 121.0 jit_solution(15675385401940018500)
XLA Ops:
  0.0 0.7 broadcast_multiply_fusion.1
  0.7 1.0 fusion.8
  1.8 0.1 fusion.16
  1.9 49.8 %all_gather.4 = bf16[16,64,256]{2,1,0:T(8,128)(2,1)S(1)} all-gather(bf16[1,64,256]{2,1,0:T(8,128)(2,1)S(1)} %slice.7), channel_id=1, replica_groups=mesh['date'=16,'trade'=16,'path'=2] {'date'}, dimensions={0}, use_global_device_ids=true | all-gather | bytes 557056 | tf_op jit(solution)/shard_map/all_gather | solution.py:27
  51.7 0.0 copy-start.3
  51.8 0.1 broadcast_add_fusion.1
  51.9 0.2 broadcast_in_dim.4
  52.1 0.0 collective-permute-start
  52.1 2.9 %collective-permute-start.1 = (f32[2,64,256]{2,1,0:T(8,128)S(1)}, f32[2,64,256]{2,1,0:T(8,128)S(1)}, u32[]{:S(2)}, u32[]{:S(2)}) collective-permute-start(f32[2,64,256]{2,1,0:T(8,128)S(1)} %get-tuple-element.38), channel_id=1, source_target_pairs={{0,30},{2,0},{4,2},{6,4},{8,6},{10,8},{12,10},{14,12},{16,14},{18,... | collective-permute-start | bytes 393224 | tf_op jit(solution)/shard_map/ppermute | solution.py:18
  55.1 0.1 compare_convert_fusion
  55.2 2.6 %collective-permute-done = f32[2,64,256]{2,1,0:T(8,128)S(1)} collective-permute-done((f32[2,64,256]{2,1,0:T(8,128)S(1)}, f32[2,64,256]{2,1,0:T(8,128)S(1)}, u32[]{:S(2)}, u32[]{:S(2)}) %collective-permute-start) | collective-permute-done | bytes 131104 | tf_op jit(solution)/shard_map/ppermute | solution.py:15
  57.7 0.0 collective-permute-start.2
  57.7 0.0 collective-permute-done.1
  57.7 3.0 %collective-permute-start.3 = (f32[2,64,256]{2,1,0:T(8,128)S(1)}, f32[2,64,256]{2,1,0:T(8,128)S(1)}, u32[]{:S(2)}, u32[]{:S(2)}) collective-permute-start(f32[2,64,256]{2,1,0:T(8,128)S(1)} %collective-permute-done.1), channel_id=1, source_target_pairs={{0,30},{2,0},{4,2},{6,4},{8,6},{10,8},{12,10},{14,12},{16,14},{18,... | collective-permute-start | bytes 393224 | tf_op jit(solution)/shard_map/ppermute | solution.py:18
  60.7 2.6 %collective-permute-done.2 = f32[2,64,256]{2,1,0:T(8,128)S(1)} collective-permute-done((f32[2,64,256]{2,1,0:T(8,128)S(1)}, f32[2,64,256]{2,1,0:T(8,128)S(1)}, u32[]{:S(2)}, u32[]{:S(2)}) %collective-permute-start.2) | collective-permute-done | bytes 131104 | tf_op jit(solution)/shard_map/ppermute | solution.py:15
  63.3 3.0 %collective-permute-start.5 = (f32[2,64,256]{2,1,0:T(8,128)S(1)}, f32[2,64,256]{2,1,0:T(8,128)S(1)}, u32[]{:S(2)}, u32[]{:S(2)}) collective-permute-start(f32[2,64,256]{2,1,0:T(8,128)S(1)} %collective-permute-done.3), channel_id=1, source_target_pairs={{0,30},{2,0},{4,2},{6,4},{8,6},{10,8},{12,10},{14,12},{16,14},{18,... | collective-permute-start | bytes 393224 | tf_op jit(solution)/shard_map/ppermute | solution.py:18
  66.3 2.6 %collective-permute-done.4 = f32[2,64,256]{2,1,0:T(8,128)S(1)} collective-permute-done((f32[2,64,256]{2,1,0:T(8,128)S(1)}, f32[2,64,256]{2,1,0:T(8,128)S(1)}, u32[]{:S(2)}, u32[]{:S(2)}) %collective-permute-start.4) | collective-permute-done | bytes 131104 | tf_op jit(solution)/shard_map/ppermute | solution.py:15
  68.9 0.0 collective-permute-start.6
  68.9 0.0 collective-permute-done.5
  68.9 3.0 %collective-permute-start.7 = (f32[2,64,256]{2,1,0:T(8,128)S(1)}, f32[2,64,256]{2,1,0:T(8,128)S(1)}, u32[]{:S(2)}, u32[]{:S(2)}) collective-permute-start(f32[2,64,256]{2,1,0:T(8,128)S(1)} %collective-permute-done.5), channel_id=1, source_target_pairs={{0,30},{2,0},{4,2},{6,4},{8,6},{10,8},{12,10},{14,12},{16,14},{18,... | collective-permute-start | bytes 393224 | tf_op jit(solution)/shard_map/ppermute | solution.py:18
  71.9 2.6 %collective-permute-done.6 = f32[2,64,256]{2,1,0:T(8,128)S(1)} collective-permute-done((f32[2,64,256]{2,1,0:T(8,128)S(1)}, f32[2,64,256]{2,1,0:T(8,128)S(1)}, u32[]{:S(2)}, u32[]{:S(2)}) %collective-permute-start.6) | collective-permute-done | bytes 131104 | tf_op jit(solution)/shard_map/ppermute | solution.py:15
  74.5 3.0 %collective-permute-start.9 = (f32[2,64,256]{2,1,0:T(8,128)S(1)}, f32[2,64,256]{2,1,0:T(8,128)S(1)}, u32[]{:S(2)}, u32[]{:S(2)}) collective-permute-start(f32[2,64,256]{2,1,0:T(8,128)S(1)} %collective-permute-done.7), channel_id=1, source_target_pairs={{0,30},{2,0},{4,2},{6,4},{8,6},{10,8},{12,10},{14,12},{16,14},{18,... | collective-permute-start | bytes 393224 | tf_op jit(solution)/shard_map/ppermute | solution.py:18
  77.5 2.6 %collective-permute-done.8 = f32[2,64,256]{2,1,0:T(8,128)S(1)} collective-permute-done((f32[2,64,256]{2,1,0:T(8,128)S(1)}, f32[2,64,256]{2,1,0:T(8,128)S(1)}, u32[]{:S(2)}, u32[]{:S(2)}) %collective-permute-start.8) | collective-permute-done | bytes 131104 | tf_op jit(solution)/shard_map/ppermute | solution.py:15
  80.1 3.0 %collective-permute-start.11 = (f32[2,64,256]{2,1,0:T(8,128)S(1)}, f32[2,64,256]{2,1,0:T(8,128)S(1)}, u32[]{:S(2)}, u32[]{:S(2)}) collective-permute-start(f32[2,64,256]{2,1,0:T(8,128)S(1)} %collective-permute-done.9), channel_id=1, source_target_pairs={{0,30},{2,0},{4,2},{6,4},{8,6},{10,8},{12,10},{14,12},{16,14},{18,... | collective-permute-start | bytes 393224 | tf_op jit(solution)/shard_map/ppermute | solution.py:18
  83.1 2.6 %collective-permute-done.10 = f32[2,64,256]{2,1,0:T(8,128)S(1)} collective-permute-done((f32[2,64,256]{2,1,0:T(8,128)S(1)}, f32[2,64,256]{2,1,0:T(8,128)S(1)}, u32[]{:S(2)}, u32[]{:S(2)}) %collective-permute-start.10) | collective-permute-done | bytes 131104 | tf_op jit(solution)/shard_map/ppermute | solution.py:15
  85.7 3.0 %collective-permute-start.13 = (f32[2,64,256]{2,1,0:T(8,128)S(1)}, f32[2,64,256]{2,1,0:T(8,128)S(1)}, u32[]{:S(2)}, u32[]{:S(2)}) collective-permute-start(f32[2,64,256]{2,1,0:T(8,128)S(1)} %collective-permute-done.11), channel_id=1, source_target_pairs={{0,30},{2,0},{4,2},{6,4},{8,6},{10,8},{12,10},{14,12},{16,14},{18,... | collective-permute-start | bytes 393224 | tf_op jit(solution)/shard_map/ppermute | solution.py:18
  88.7 2.6 %collective-permute-done.12 = f32[2,64,256]{2,1,0:T(8,128)S(1)} collective-permute-done((f32[2,64,256]{2,1,0:T(8,128)S(1)}, f32[2,64,256]{2,1,0:T(8,128)S(1)}, u32[]{:S(2)}, u32[]{:S(2)}) %collective-permute-start.12) | collective-permute-done | bytes 131104 | tf_op jit(solution)/shard_map/ppermute | solution.py:15
  91.4 5.5 %collective-permute-done.14 = f32[2,64,256]{2,1,0:T(8,128)S(1)} collective-permute-done((f32[2,64,256]{2,1,0:T(8,128)S(1)}, f32[2,64,256]{2,1,0:T(8,128)S(1)}, u32[]{:S(2)}, u32[]{:S(2)}) %collective-permute-start.14) | collective-permute-done | bytes 131104 | tf_op jit(solution)/shard_map/ppermute | solution.py:15
  97.0 7.9 %fusion.6 = bf16[2,4096,128]{2,1,0:T(8,128)(2,1)} fusion(f32[2,64,4096]{2,1,0:T(8,128)S(1)} %constant_dynamic-update-slice_fusion, f32[128]{0:T(128)S(1)} %copy-done.5, f32[64,128]{1,0:T(8,128)S(1)} %copy-done.1), kind=kOutput, calls=%fused_computation.8 | convolution fusion | flops 807403520 | bytes 4227584 | tf_op jit(solution)/shard_map/tfp,fk->tpk/dot_general | solution.py:65
  104.9 10.6 %fusion.7 = f32[2,128]{1,0:T(2,128)S(1)} fusion(f32[2,1024]{1,0:T(2,128)S(1)} %compare_convert_fusion, bf16[2,4096,128]{2,1,0:T(8,128)(2,1)} %fusion.6, bf16[128,1024]{1,0:T(8,128)(2,1)S(1)} %copy-done, s32[1024]{0:T(1024)S(1)} %broadcast_subtract_fusion), kind=kOutput, calls=%fused_computation.9 | convolution fusion | flops 4313972736 | bytes 2372608 | tf_op jit(solution)/shard_map/tpj,js->tps/dot_general | solution.py:71
  115.5 4.9 %psum.7 = f32[2,128]{1,0:T(2,128)S(1)} all-reduce(f32[2,128]{1,0:T(2,128)S(1)} %fusion.7), channel_id=1, replica_groups=mesh['date'=16,'trade'=16,'path'=2] {'path'}, use_global_device_ids=true, to_apply=%region_4.5 | all-reduce | flops 256 | bytes 2048 | tf_op jit(solution)/shard_map/psum | solution.py:73
  120.4 0.6 broadcast_multiply_fusion
  (42 shorter events, 0.3 us)
Async XLA Ops:
  0.0 104.9 %copy-start = (bf16[128,1024]{1,0:T(8,128)(2,1)S(1)}, bf16[128,1024]{1,0:T(8,128)(2,1)}, u32[]{:S(2)}) copy-start(bf16[128,1024]{1,0:T(8,128)(2,1)} %param.17) | copy-start | bytes 786436
  0.0 51.8 %copy-start.4 = (f32[64]{0:T(128)S(1)}, f32[64]{0:T(128)}, u32[]{:S(2)}) copy-start(f32[64]{0:T(128)} %param.14) | copy-start | bytes 772
  51.7 3.3 %copy-start.2 = (s32[1024]{0:T(1024)S(1)}, s32[1024]{0:T(1024)}, u32[]{:S(2)}) copy-start(s32[1024]{0:T(1024)} %param.18) | copy-start | bytes 12292
  51.7 3.4 %copy-start.3 = (s32[1024]{0:T(1024)S(1)}, s32[1024]{0:T(1024)}, u32[]{:S(2)}) copy-start(s32[1024]{0:T(1024)} %param.19) | copy-start | bytes 12292
  52.1 5.6 %collective-permute-start = (f32[2,64,256]{2,1,0:T(8,128)S(1)}, f32[2,64,256]{2,1,0:T(8,128)S(1)}, u32[]{:S(2)}, u32[]{:S(2)}) collective-permute-start(f32[2,64,256]{2,1,0:T(8,128)S(1)} %get-tuple-element.38), channel_id=1, source_target_pairs={{0,2},{2,4},{4,6},{6,8},{8,10},{10,12},{12,14},{14,16},{16,18},{18... | collective-permute-start | bytes 393224 | tf_op jit(solution)/shard_map/ppermute | solution.py:15
  52.1 5.6 %collective-permute-start.1 = (f32[2,64,256]{2,1,0:T(8,128)S(1)}, f32[2,64,256]{2,1,0:T(8,128)S(1)}, u32[]{:S(2)}, u32[]{:S(2)}) collective-permute-start(f32[2,64,256]{2,1,0:T(8,128)S(1)} %get-tuple-element.38), channel_id=1, source_target_pairs={{0,30},{2,0},{4,2},{6,4},{8,6},{10,8},{12,10},{14,12},{16,14},{18,... | collective-permute-start | bytes 393224 | tf_op jit(solution)/shard_map/ppermute | solution.py:18
  55.1 41.9 %copy-start.1 = (f32[64,128]{1,0:T(8,128)S(1)}, f32[64,128]{1,0:T(8,128)}, u32[]{:S(2)}) copy-start(f32[64,128]{1,0:T(8,128)} %param.15) | copy-start | bytes 98308
  55.1 41.9 %copy-start.5 = (f32[128]{0:T(128)S(1)}, f32[128]{0:T(128)}, u32[]{:S(2)}) copy-start(f32[128]{0:T(128)} %param.16) | copy-start | bytes 1540
  57.7 5.6 %collective-permute-start.2 = (f32[2,64,256]{2,1,0:T(8,128)S(1)}, f32[2,64,256]{2,1,0:T(8,128)S(1)}, u32[]{:S(2)}, u32[]{:S(2)}) collective-permute-start(f32[2,64,256]{2,1,0:T(8,128)S(1)} %collective-permute-done), channel_id=1, source_target_pairs={{0,2},{2,4},{4,6},{6,8},{8,10},{10,12},{12,14},{14,16},{16,18},{18... | collective-permute-start | bytes 393224 | tf_op jit(solution)/shard_map/ppermute | solution.py:15
  57.7 5.6 %collective-permute-start.3 = (f32[2,64,256]{2,1,0:T(8,128)S(1)}, f32[2,64,256]{2,1,0:T(8,128)S(1)}, u32[]{:S(2)}, u32[]{:S(2)}) collective-permute-start(f32[2,64,256]{2,1,0:T(8,128)S(1)} %collective-permute-done.1), channel_id=1, source_target_pairs={{0,30},{2,0},{4,2},{6,4},{8,6},{10,8},{12,10},{14,12},{16,14},{18,... | collective-permute-start | bytes 393224 | tf_op jit(solution)/shard_map/ppermute | solution.py:18
  63.3 5.6 %collective-permute-start.4 = (f32[2,64,256]{2,1,0:T(8,128)S(1)}, f32[2,64,256]{2,1,0:T(8,128)S(1)}, u32[]{:S(2)}, u32[]{:S(2)}) collective-permute-start(f32[2,64,256]{2,1,0:T(8,128)S(1)} %collective-permute-done.2), channel_id=1, source_target_pairs={{0,2},{2,4},{4,6},{6,8},{8,10},{10,12},{12,14},{14,16},{16,18},{18... | collective-permute-start | bytes 393224 | tf_op jit(solution)/shard_map/ppermute | solution.py:15
  63.3 5.6 %collective-permute-start.5 = (f32[2,64,256]{2,1,0:T(8,128)S(1)}, f32[2,64,256]{2,1,0:T(8,128)S(1)}, u32[]{:S(2)}, u32[]{:S(2)}) collective-permute-start(f32[2,64,256]{2,1,0:T(8,128)S(1)} %collective-permute-done.3), channel_id=1, source_target_pairs={{0,30},{2,0},{4,2},{6,4},{8,6},{10,8},{12,10},{14,12},{16,14},{18,... | collective-permute-start | bytes 393224 | tf_op jit(solution)/shard_map/ppermute | solution.py:18
  68.9 5.6 %collective-permute-start.6 = (f32[2,64,256]{2,1,0:T(8,128)S(1)}, f32[2,64,256]{2,1,0:T(8,128)S(1)}, u32[]{:S(2)}, u32[]{:S(2)}) collective-permute-start(f32[2,64,256]{2,1,0:T(8,128)S(1)} %collective-permute-done.4), channel_id=1, source_target_pairs={{0,2},{2,4},{4,6},{6,8},{8,10},{10,12},{12,14},{14,16},{16,18},{18... | collective-permute-start | bytes 393224 | tf_op jit(solution)/shard_map/ppermute | solution.py:15
  68.9 5.6 %collective-permute-start.7 = (f32[2,64,256]{2,1,0:T(8,128)S(1)}, f32[2,64,256]{2,1,0:T(8,128)S(1)}, u32[]{:S(2)}, u32[]{:S(2)}) collective-permute-start(f32[2,64,256]{2,1,0:T(8,128)S(1)} %collective-permute-done.5), channel_id=1, source_target_pairs={{0,30},{2,0},{4,2},{6,4},{8,6},{10,8},{12,10},{14,12},{16,14},{18,... | collective-permute-start | bytes 393224 | tf_op jit(solution)/shard_map/ppermute | solution.py:18
  74.5 5.6 %collective-permute-start.8 = (f32[2,64,256]{2,1,0:T(8,128)S(1)}, f32[2,64,256]{2,1,0:T(8,128)S(1)}, u32[]{:S(2)}, u32[]{:S(2)}) collective-permute-start(f32[2,64,256]{2,1,0:T(8,128)S(1)} %collective-permute-done.6), channel_id=1, source_target_pairs={{0,2},{2,4},{4,6},{6,8},{8,10},{10,12},{12,14},{14,16},{16,18},{18... | collective-permute-start | bytes 393224 | tf_op jit(solution)/shard_map/ppermute | solution.py:15
  74.5 5.6 %collective-permute-start.9 = (f32[2,64,256]{2,1,0:T(8,128)S(1)}, f32[2,64,256]{2,1,0:T(8,128)S(1)}, u32[]{:S(2)}, u32[]{:S(2)}) collective-permute-start(f32[2,64,256]{2,1,0:T(8,128)S(1)} %collective-permute-done.7), channel_id=1, source_target_pairs={{0,30},{2,0},{4,2},{6,4},{8,6},{10,8},{12,10},{14,12},{16,14},{18,... | collective-permute-start | bytes 393224 | tf_op jit(solution)/shard_map/ppermute | solution.py:18
  80.1 5.6 %collective-permute-start.10 = (f32[2,64,256]{2,1,0:T(8,128)S(1)}, f32[2,64,256]{2,1,0:T(8,128)S(1)}, u32[]{:S(2)}, u32[]{:S(2)}) collective-permute-start(f32[2,64,256]{2,1,0:T(8,128)S(1)} %collective-permute-done.8), channel_id=1, source_target_pairs={{0,2},{2,4},{4,6},{6,8},{8,10},{10,12},{12,14},{14,16},{16,18},{18... | collective-permute-start | bytes 393224 | tf_op jit(solution)/shard_map/ppermute | solution.py:15
  80.1 5.6 %collective-permute-start.11 = (f32[2,64,256]{2,1,0:T(8,128)S(1)}, f32[2,64,256]{2,1,0:T(8,128)S(1)}, u32[]{:S(2)}, u32[]{:S(2)}) collective-permute-start(f32[2,64,256]{2,1,0:T(8,128)S(1)} %collective-permute-done.9), channel_id=1, source_target_pairs={{0,30},{2,0},{4,2},{6,4},{8,6},{10,8},{12,10},{14,12},{16,14},{18,... | collective-permute-start | bytes 393224 | tf_op jit(solution)/shard_map/ppermute | solution.py:18
  85.7 5.6 %collective-permute-start.12 = (f32[2,64,256]{2,1,0:T(8,128)S(1)}, f32[2,64,256]{2,1,0:T(8,128)S(1)}, u32[]{:S(2)}, u32[]{:S(2)}) collective-permute-start(f32[2,64,256]{2,1,0:T(8,128)S(1)} %collective-permute-done.10), channel_id=1, source_target_pairs={{0,2},{2,4},{4,6},{6,8},{8,10},{10,12},{12,14},{14,16},{16,18},{18... | collective-permute-start | bytes 393224 | tf_op jit(solution)/shard_map/ppermute | solution.py:15
  85.7 5.6 %collective-permute-start.13 = (f32[2,64,256]{2,1,0:T(8,128)S(1)}, f32[2,64,256]{2,1,0:T(8,128)S(1)}, u32[]{:S(2)}, u32[]{:S(2)}) collective-permute-start(f32[2,64,256]{2,1,0:T(8,128)S(1)} %collective-permute-done.11), channel_id=1, source_target_pairs={{0,30},{2,0},{4,2},{6,4},{8,6},{10,8},{12,10},{14,12},{16,14},{18,... | collective-permute-start | bytes 393224 | tf_op jit(solution)/shard_map/ppermute | solution.py:18
  91.3 5.6 %collective-permute-start.14 = (f32[2,64,256]{2,1,0:T(8,128)S(1)}, f32[2,64,256]{2,1,0:T(8,128)S(1)}, u32[]{:S(2)}, u32[]{:S(2)}) collective-permute-start(f32[2,64,256]{2,1,0:T(8,128)S(1)} %collective-permute-done.12), channel_id=1, source_target_pairs={{0,2},{2,4},{4,6},{6,8},{8,10},{10,12},{12,14},{14,16},{16,18},{18... | collective-permute-start | bytes 393224 | tf_op jit(solution)/shard_map/ppermute | solution.py:15
